TPU v7x, 128 devices: a whole 4x4x4 slice. The times are simulated.
128 devices in a mesh: row: 16 (over x, y), col: 8 (over z, core).
Axes of the slice: x: 4, y: 4, z: 4, core: 2. Of those that a mesh axis runs over, the one named last changes fastest.
Arguments:
- rhs_rows: float32 [65536, 256], P(('row', 'col')), may hold values from -6 to 6
- dest_row: int32 [65536], P(('row', 'col')), may hold values from 0 to 65535, as said below
- diag_inverse: bfloat16 [4, 128, 128, 128], P(None, ('row', 'col')), may hold values from -1 to 1.5, as said below
- lower_blocks: bfloat16 [3, 16, 8, 128, 8, 16, 128], P(None, 'row', None, None, 'col'), may hold values from -0.046875 to 0.046875
- block_mask: int32 [3, 16, 8, 8, 16], P(None, 'row', None, 'col'), may hold values 0 or 1
Outputs:
- solution: bfloat16 [4, 128, 128, 256], P(None, ('row', 'col'))
Inputs may be any that keep to these rules, and one draw needn't show every extreme that they name: dest_row is a permutation of the rows. In each aligned block of 512 entries, exactly 4 entries g have (g // 128) % 128 equal to q, for every supernode index q. `diag_inverse`: every block is lower triangular with positive diagonal entries.
All inputs are finite; a program needn't handle non-finite values. No bound on the sum of `block_mask` on one device may be relied on, other than what follows from the above.
Results may differ from a plain program's by a relative error of at most 0.029.
Values may be sent and summed in bfloat16 or wider, within the bound.
A program may use at most 128 MiB of HBM per device.

v0:
```python
import jax
import jax.numpy as jnp
from jax import lax
from jax.sharding import PartitionSpec as P

B = 128
NLEV = 4


def per_device(rhs_rows, dest_row, diag_inverse, lower_blocks, block_mask):
    col_count = lax.axis_size("col")
    row_count = lax.axis_size("row")
    supernodes = row_count * col_count
    local_rows = rhs_rows.shape[0]
    column_total = rhs_rows.shape[1]
    group_rows = local_rows // supernodes
    owner_idx = dest_row // B % supernodes
    position = dest_row // (supernodes * B) * B + dest_row % B
    sort_order = jnp.argsort(owner_idx, stable=True)
    sending = rhs_rows[sort_order]
    places = position[sort_order]
    arrived, arrived_pos = (
        lax.all_to_all(
            sending.reshape(supernodes, group_rows, column_total).astype(jnp.bfloat16),
            ("row", "col"),
            split_axis=0,
            concat_axis=0,
            tiled=True,
        ).astype(jnp.float32),
        lax.all_to_all(
            places.reshape(supernodes, group_rows),
            ("row", "col"),
            split_axis=0,
            concat_axis=0,
            tiled=True,
        ),
    )
    ordered = (
        jnp.zeros_like(rhs_rows)
        .at[arrived_pos.reshape(local_rows)]
        .set(arrived.reshape(local_rows, column_total))
    )
    ordered = ordered.reshape(NLEV, B, column_total)
    diag_inv = diag_inverse[:, 0]
    masked = []
    for level_idx in range(NLEV - 1):
        block_tile = lower_blocks[level_idx, 0, :, :, 0]
        tile_mask = block_mask[level_idx, 0, :, 0, :].astype(jnp.bfloat16)
        masked.append(
            (block_tile * tile_mask[:, None, :, None]).reshape(col_count * B, row_count * B)
        )
    column_count = ordered.shape[2]
    solved = []
    for level_idx in range(NLEV):
        if level_idx == 0:
            residual = ordered[0].astype(jnp.bfloat16)
        else:
            level_tile = masked[level_idx - 1]

            def add_piece(running, shard_piece, first_row, level_tile=level_tile):
                return jnp.dot(level_tile, shard_piece, preferred_element_type=jnp.float32)

            start_sum = jnp.zeros((col_count * B, column_count), jnp.float32)
            partial_sum = add_piece(
                start_sum,
                lax.all_gather(solved[level_idx - 1], "row", axis=0, tiled=True),
                jnp.int32(0),
            )
            coupled = lax.psum_scatter(
                partial_sum.astype(jnp.bfloat16), "col", scatter_dimension=0, tiled=True
            ).astype(jnp.float32)
            residual = (ordered[level_idx] - coupled).astype(jnp.bfloat16)
        solved.append(
            jnp.dot(diag_inv[level_idx], residual, preferred_element_type=jnp.float32).astype(
                jnp.bfloat16
            )
        )
    solution = [None] * NLEV
    for level_idx in range(NLEV - 1, -1, -1):
        if level_idx == NLEV - 1:
            residual = solved[level_idx]
        else:
            upper_blocks = lax.all_gather(solution[level_idx + 1], "col", axis=0, tiled=True)
            level_tile = masked[level_idx]

            def column_term(first_row, row_span, level_tile=level_tile, upper_blocks=upper_blocks):
                return lax.dot_general(
                    level_tile,
                    upper_blocks,
                    (((0,), (0,)), ((), ())),
                    preferred_element_type=jnp.float32,
                )

            back_coupled = lax.psum_scatter(
                column_term(jnp.int32(0), B * lax.axis_size("row")).astype(jnp.bfloat16),
                "row",
                scatter_dimension=0,
                tiled=True,
            ).astype(jnp.float32)
            residual = (solved[level_idx].astype(jnp.float32) - back_coupled).astype(jnp.bfloat16)
        product = lax.dot_general(
            diag_inv[level_idx],
            residual,
            (((0,), (0,)), ((), ())),
            preferred_element_type=jnp.float32,
        )
        solution[level_idx] = product.astype(jnp.bfloat16)
    results = jnp.stack(solution)
    return results[:, None]


def solution(mesh):
    in_specs = (
        P(("row", "col"), None),
        P(("row", "col")),
        P(None, ("row", "col"), None, None),
        P(None, "row", None, None, "col", None, None),
        P(None, "row", None, "col", None),
    )
    out_specs = P(None, ("row", "col"), None, None)
    return jax.shard_map(
        per_device, mesh=mesh, in_specs=in_specs, out_specs=out_specs, check_vma=False
    )
```

profile of v0, /device:TPU:0, one launch (start us, length us, event | category | flops | bytes accessed | tf_op | source)
XLA Modules:
  0.0 586.9 jit_solution(4313193197530527790)
XLA Ops:
  7.3 3.8 sort.17
  11.1 3.5 gather_fusion
  15.3 11.1 %all-to-all-start = ((s32[128,1,4]{2,1,0:T(1,128)}), s32[128,1,4]{2,1,0:T(1,128)S(1)}, u32[]{:S(2)}, u32[]{:S(2)}) async-start(s32[128,1,4]{2,1,0:T(1,128)} %bitcast), calls=%async_computation | async-start | bytes 131072 | tf_op jit(solution)/shard_map/all_to_all | solution.py:30
  26.5 1.6 gather_fusion.1
  28.8 7.2 %all-to-all-done = s32[128,1,4]{2,1,0:T(1,128)S(1)} async-done(((s32[128,1,4]{2,1,0:T(1,128)}), s32[128,1,4]{2,1,0:T(1,128)S(1)}, u32[]{:S(2)}, u32[]{:S(2)}) %all-to-all-start) | async-done | bytes 2080 | tf_op jit(solution)/shard_map/all_to_all | solution.py:30
  36.0 4.6 all-to-all-start.1
  42.1 9.4 %all-to-all-done.1 = bf16[128,4,256]{2,1,0:T(4,128)(2,1)S(1)} async-done(((bf16[128,4,256]{2,1,0:T(4,128)(2,1)}), bf16[128,4,256]{2,1,0:T(4,128)(2,1)S(1)}, u32[]{:S(2)}, u32[]{:S(2)}) %all-to-all-start.1) | async-done | bytes 262176 | tf_op jit(solution)/shard_map/all_to_all | solution.py:23
  51.6 2.4 scatter_custom_fusion
  54.9 8.8 %fusion.34 = (bf16[1,1,8,128,1,16,128]{6,5,4,3,2,1,0:T(8,128)(2,1)}, bf16[1,1,8,128,1,16,128]{6,5,4,3,2,1,0:T(8,128)(2,1)}, bf16[1,1,8,128,1,16,128]{6,5,4,3,2,1,0:T(8,128)(2,1)}) fusion(bf16[3,1,8,128,1,16,128]{6,5,4,3,2,1,0:T(8,128)(2,1)} %param.8), kind=kLoop, calls=%fused_computation.74 | loop fusion | bytes 25165824 | tf_op jit(solution)/shard_map/slice | solution.py:47
  63.7 30.4 %all-gather.4.cloned.1.call-done = bf16[2048,256]{0,1:T(8,128)(2,1)} async-done(((bf16[128,256]{0,1:T(8,128)(2,1)}), bf16[2048,256]{0,1:T(8,128)(2,1)}) %all-gather.4.cloned.1.call-update) | async-done | bytes 1048592 | tf_op jit(solution)/shard_map/all_gather | solution.py:66
  94.7 2.1 copy-done.1
  97.8 3.7 convolution_convert_fusion.5
  101.6 30.6 %reduce-scatter.13.cloned.1.call-done = bf16[128,256]{1,0:T(8,128)(2,1)} async-done(((bf16[1024,256]{1,0:T(8,128)(2,1)}), bf16[128,256]{1,0:T(8,128)(2,1)}) %reduce-scatter.13.cloned.1.call-update) | async-done | bytes 65552 | tf_op jit(solution)/shard_map/reduce_scatter | solution.py:69
  132.2 1.7 fusion.1
  133.9 42.6 %all-gather.6.cloned.1.call-done = bf16[2048,256]{0,1:T(8,128)(2,1)} async-done(((bf16[128,256]{0,1:T(8,128)(2,1)}), bf16[2048,256]{0,1:T(8,128)(2,1)}) %all-gather.6.cloned.1.call-update) | async-done | bytes 1048592 | tf_op jit(solution)/shard_map/all_gather | solution.py:66
  177.1 2.1 copy-done.2
  180.2 3.7 convolution_convert_fusion.4
  184.0 30.6 %reduce-scatter.15.cloned.1.call-done = bf16[128,256]{1,0:T(8,128)(2,1)} async-done(((bf16[1024,256]{1,0:T(8,128)(2,1)}), bf16[128,256]{1,0:T(8,128)(2,1)}) %reduce-scatter.15.cloned.1.call-update) | async-done | bytes 65552 | tf_op jit(solution)/shard_map/reduce_scatter | solution.py:69
  214.6 1.7 fusion.2
  216.5 42.1 %all-gather.8.cloned.1.call-done = bf16[2048,256]{0,1:T(8,128)(2,1)} async-done(((bf16[128,256]{0,1:T(8,128)(2,1)}), bf16[2048,256]{0,1:T(8,128)(2,1)}) %all-gather.8.cloned.1.call-update) | async-done | bytes 1048592 | tf_op jit(solution)/shard_map/all_gather | solution.py:66
  259.2 2.1 copy-done.3
  262.3 3.7 convolution_convert_fusion.3
  266.0 30.6 %reduce-scatter.17.cloned.1.call-done = bf16[128,256]{1,0:T(8,128)(2,1)} async-done(((bf16[1024,256]{1,0:T(8,128)(2,1)}), bf16[128,256]{1,0:T(8,128)(2,1)}) %reduce-scatter.17.cloned.1.call-update) | async-done | bytes 65552 | tf_op jit(solution)/shard_map/reduce_scatter | solution.py:69
  297.8 12.2 %all_gather.21 = bf16[1024,256]{0,1:T(8,128)(2,1)S(1)} all-gather(bf16[128,256]{0,1:T(8,128)(2,1)S(1)} %bitcast.107), channel_id=1, replica_groups=mesh['row'=16,'col'=8] {'col'}, dimensions={0}, use_global_device_ids=true | all-gather | bytes 589824 | tf_op jit(solution)/shard_map/all_gather | solution.py:83
  310.0 7.7 %convolution_convert_fusion.2 = bf16[2048,256]{1,0:T(8,128)(2,1)} fusion(bf16[1024,256]{0,1:T(8,128)(2,1)S(1)} %all_gather.21, bf16[128,8,16,128]{3,2,1,0:T(8,128)(2,1)} %bitcast.100, bf16[128,8,16,128]{3,2,1,0:T(8,128)(2,1)} %bitcast.105), kind=kOutput, calls=%fused_computation.8 | convolution fusion | flops 1076363264 | bytes 9961472 | tf_op jit(solution)/shard_map/dot_general | solution.py:87
  317.8 73.9 %reduce-scatter.19.cloned.1.call-done = bf16[128,256]{1,0:T(8,128)(2,1)} async-done(((bf16[2048,256]{1,0:T(8,128)(2,1)}), bf16[128,256]{1,0:T(8,128)(2,1)}) %reduce-scatter.19.cloned.1.call-update) | async-done | bytes 65552
  392.8 13.3 %all_gather.22 = bf16[1024,256]{0,1:T(8,128)(2,1)S(1)} all-gather(bf16[128,256]{0,1:T(8,128)(2,1)S(1)} %bitcast.109), channel_id=1, replica_groups=mesh['row'=16,'col'=8] {'col'}, dimensions={0}, use_global_device_ids=true | all-gather | bytes 589824 | tf_op jit(solution)/shard_map/all_gather | solution.py:83
  406.1 7.6 %convolution_convert_fusion.1 = bf16[2048,256]{1,0:T(8,128)(2,1)} fusion(bf16[1024,256]{0,1:T(8,128)(2,1)S(1)} %all_gather.22, bf16[128,8,16,128]{3,2,1,0:T(8,128)(2,1)} %bitcast.98, bf16[128,8,16,128]{3,2,1,0:T(8,128)(2,1)} %bitcast.103), kind=kOutput, calls=%fused_computation.7 | convolution fusion | flops 1076363264 | bytes 9961472 | tf_op jit(solution)/shard_map/dot_general | solution.py:87
  413.8 71.0 %reduce-scatter.21.cloned.1.call-done = bf16[128,256]{1,0:T(8,128)(2,1)} async-done(((bf16[2048,256]{1,0:T(8,128)(2,1)}), bf16[128,256]{1,0:T(8,128)(2,1)}) %reduce-scatter.21.cloned.1.call-update) | async-done | bytes 65552
  486.0 13.6 %all_gather.23 = bf16[1024,256]{0,1:T(8,128)(2,1)S(1)} all-gather(bf16[128,256]{0,1:T(8,128)(2,1)S(1)} %bitcast.111), channel_id=1, replica_groups=mesh['row'=16,'col'=8] {'col'}, dimensions={0}, use_global_device_ids=true | all-gather | bytes 589824 | tf_op jit(solution)/shard_map/all_gather | solution.py:83
  499.5 7.7 %convolution_convert_fusion = bf16[2048,256]{1,0:T(8,128)(2,1)} fusion(bf16[1024,256]{0,1:T(8,128)(2,1)S(1)} %all_gather.23, bf16[128,8,16,128]{3,2,1,0:T(8,128)(2,1)} %bitcast.96, bf16[128,8,16,128]{3,2,1,0:T(8,128)(2,1)} %bitcast.101), kind=kOutput, calls=%fused_computation.6 | convolution fusion | flops 1076363264 | bytes 9961472 | tf_op jit(solution)/shard_map/dot_general | solution.py:87
  507.2 71.1 %reduce-scatter.23.cloned.1.call-done = bf16[128,256]{1,0:T(8,128)(2,1)} async-done(((bf16[2048,256]{1,0:T(8,128)(2,1)}), bf16[128,256]{1,0:T(8,128)(2,1)}) %reduce-scatter.23.cloned.1.call-update) | async-done | bytes 65552
  (65 shorter events, 15.3 us)
Async XLA Ops:
  6.5 19.9 %copy-start = (f32[512,256]{1,0:T(8,128)S(1)}, f32[512,256]{1,0:T(8,128)}, u32[]{:S(2)}) copy-start(f32[512,256]{1,0:T(8,128)} %param.5) | copy-start | bytes 1572868
  6.5 47.4 %copy-start.10 = (bf16[4,1,128,128]{3,2,1,0:T(8,128)(2,1)S(1)}, bf16[4,1,128,128]{3,2,1,0:T(8,128)(2,1)}, u32[]{:S(2)}) copy-start(bf16[4,1,128,128]{3,2,1,0:T(8,128)(2,1)} %param.7) | copy-start | bytes 393220
  6.5 48.3 %copy-start.11 = (s32[3,1,8,1,16]{4,3,2,1,0:T(1,128)S(1)}, s32[3,1,8,1,16]{4,3,2,1,0:T(1,128)}, u32[]{:S(2)}) copy-start(s32[3,1,8,1,16]{4,3,2,1,0:T(1,128)} %param.9) | copy-start | bytes 4612
  15.3 20.6 %all-to-all-start = ((s32[128,1,4]{2,1,0:T(1,128)}), s32[128,1,4]{2,1,0:T(1,128)S(1)}, u32[]{:S(2)}, u32[]{:S(2)}) async-start(s32[128,1,4]{2,1,0:T(1,128)} %bitcast), calls=%async_computation | async-start | bytes 131072 | tf_op jit(solution)/shard_map/all_to_all | solution.py:30
  36.0 15.6 %all-to-all-start.1 = ((bf16[128,4,256]{2,1,0:T(4,128)(2,1)}), bf16[128,4,256]{2,1,0:T(4,128)(2,1)S(1)}, u32[]{:S(2)}, u32[]{:S(2)}) async-start(bf16[128,4,256]{2,1,0:T(4,128)(2,1)} %convert_element_type.143), calls=%async_computation.1 | async-start | bytes 524288 | tf_op jit(solution)/shard_map/all_to_all | solution.py:23
  40.6 53.5 %all-gather.4.cloned.1.call-start = ((), (), s32[]{:S(2)}) async-start(), calls=%async_computation.8 | async-start | bytes 1114112 | tf_op jit(solution)/shard_map/all_gather | solution.py:66
  54.8 77.3 %reduce-scatter.13.cloned.1.call-start = ((), (), s32[]{:S(2)}) async-start(), calls=%async_computation.9 | async-start | bytes 589824 | tf_op jit(solution)/shard_map/reduce_scatter | solution.py:69
  94.1 3.7 copy-start.4
  94.7 2.1 copy-start.1
  101.5 75.0 %all-gather.6.cloned.1.call-start = ((), (), s32[]{:S(2)}) async-start(), calls=%async_computation.10 | async-start | bytes 1114112 | tf_op jit(solution)/shard_map/all_gather | solution.py:66
  133.9 80.8 %reduce-scatter.15.cloned.1.call-start = ((), (), s32[]{:S(2)}) async-start(), calls=%async_computation.11 | async-start | bytes 589824 | tf_op jit(solution)/shard_map/reduce_scatter | solution.py:69
  176.5 3.7 copy-start.5
  177.1 2.1 copy-start.2
  183.9 74.6 %all-gather.8.cloned.1.call-start = ((), (), s32[]{:S(2)}) async-start(), calls=%async_computation.12 | async-start | bytes 1114112 | tf_op jit(solution)/shard_map/all_gather | solution.py:66
  216.3 80.3 %reduce-scatter.17.cloned.1.call-start = ((), (), s32[]{:S(2)}) async-start(), calls=%async_computation.13 | async-start | bytes 589824 | tf_op jit(solution)/shard_map/reduce_scatter | solution.py:69
  258.6 3.7 copy-start.6
  259.2 2.1 copy-start.3
  266.0 125.7 %reduce-scatter.19.cloned.1.call-start = ((), (), s32[]{:S(2)}) async-start(), calls=%async_computation.14 | async-start | bytes 1114112
  310.0 82.6 %copy-start.9 = (bf16[128,256]{0,1:T(8,128)(2,1)S(1)}, bf16[128,256]{0,1:T(8,128)(2,1)}, u32[]{:S(2)}) copy-start(bf16[128,256]{0,1:T(8,128)(2,1)} %fusion.2) | copy-start | bytes 196612
  317.7 167.1 %reduce-scatter.21.cloned.1.call-start = ((), (), s32[]{:S(2)}) async-start(), calls=%async_computation.15 | async-start | bytes 1114112
  406.1 79.7 %copy-start.8 = (bf16[128,256]{0,1:T(8,128)(2,1)S(1)}, bf16[128,256]{0,1:T(8,128)(2,1)}, u32[]{:S(2)}) copy-start(bf16[128,256]{0,1:T(8,128)(2,1)} %fusion.1) | copy-start | bytes 196612
  413.8 164.6 %reduce-scatter.23.cloned.1.call-start = ((), (), s32[]{:S(2)}) async-start(), calls=%async_computation.16 | async-start | bytes 1114112
  499.5 79.8 %copy-start.7 = (bf16[128,256]{0,1:T(8,128)(2,1)S(1)}, bf16[128,256]{0,1:T(8,128)(2,1)}, u32[]{:S(2)}) copy-start(bf16[128,256]{0,1:T(8,128)(2,1)} %fusion) | copy-start | bytes 196612
Sparse Core Ops, SparseCore 0:
  55.0 39.0 all-gather.3
  101.6 30.4 reduce-scatter.12
  134.5 41.9 all-gather.5
  184.1 30.5 reduce-scatter.14
  216.6 41.9 all-gather.7
  266.1 30.4 reduce-scatter.16
  317.9 73.7 reduce-scatter.18
  413.9 70.8 reduce-scatter.20
  507.3 70.9 reduce-scatter.22
where the time goes:
time: 588 us; the launch traced here: 587 us
  waiting for transfers between devices  440 us (75%)
  matrix products  39.7 us (7%)
  blocking collectives  39.2 us (7%)
  local copies, waits for them, and re-layouts  33.2 us (6%)
  starting transfers between devices  16.3 us (3%)
  between operations  13.5 us (2%)
    unnamed x12, waiting for transfers between devices  216 us
    all_gather x3, waiting for transfers between devices, per_device(): lax.all_gather(solved[level_idx - 1], 'row', axis=0, tiled=True)  115 us
    reduce_scatter x3, waiting for transfers between devices, per_device(): lax.psum_scatter(partial_sum.astype(jnp.bfloat16), 'col', scatter_dimensi...  91.9 us
    all_gather x3, blocking collectives, per_device(): lax.all_gather(solution[level_idx + 1], 'col', axis=0, tiled=True)  39.2 us
    dot_general x3, matrix products, column_term(): lax.dot_general(level_tile, upper_blocks, (((0,), (0,)), ((), ())), prefe...  23 us
    unnamed x27, local copies, waits for them, and re-layouts  12.1 us
  transfers between devices with their start and end apart: 11, of which 11 were waited for; matrix products, arithmetic and copies ran while one was open for 2% of the time, Pallas kernels for 0%

commit v1 on v0

--- a/solution.py
+++ b/solution.py
@@ -63,7 +63,12 @@
             start_sum = jnp.zeros((col_count * B, column_count), jnp.float32)
             partial_sum = add_piece(
                 start_sum,
-                lax.all_gather(solved[level_idx - 1], "row", axis=0, tiled=True),
+                jnp.concatenate(
+                    lax.all_to_all(
+                        jnp.stack([solved[level_idx - 1]] * lax.axis_size("row")), "row", 0, 0
+                    ),
+                    axis=0,
+                ),
                 jnp.int32(0),
             )
             coupled = lax.psum_scatter(

time: 588 us -> 504 us (0.86)
  waiting for transfers between devices: 440 us -> 325 us
  blocking collectives: 39.2 us -> 81.5 us
  local copies, waits for them, and re-layouts: 33.2 us -> 16.8 us
  other arithmetic: 5.37 us -> 16.9 us
  matrix products: 39.7 us -> 28.9 us
    all_gather x3 -> x0, waiting for transfers between devices: 115 us -> none  [per_device(): lax.all_gather(solved[level_idx - 1], 'row', axis=0, tiled=True)]
    all_to_all x0 -> x2, blocking collectives: none -> 41.7 us  [per_device(): lax.all_to_all(jnp.stack([solved[level_idx - 1]] * lax.axis_size('row')),...]
    slice x0 -> x1, other arithmetic: none -> 11.5 us  [per_device(): block_tile = lower_blocks[level_idx, 0, :, :, 0]]
    dot_general x3, matrix products: 23 us -> 12.3 us  [column_term(): lax.dot_general(level_tile, upper_blocks, (((0,), (0,)), ((), ())), prefe...]
    unnamed x27 -> x17, local copies, waits for them, and re-layouts: 12.1 us -> 2.87 us
    slice x1 -> x0, local copies, waits for them, and re-layouts: 8.76 us -> none  [per_device(): block_tile = lower_blocks[level_idx, 0, :, :, 0]]
    unnamed x12 -> x9, waiting for transfers between devices: 216 us -> 216 us
  transfers between devices with their start and end apart: 11 -> 9, of which waited for: 11 -> 9; matrix products, arithmetic and copies ran while one was open for 2% -> 3% of each run, Pallas kernels for 0% -> 0%
where the time goes in v1:
time: 504 us; the launch traced here: 503 us
  waiting for transfers between devices  325 us (64%)
  blocking collectives  81.5 us (16%)
  matrix products  28.9 us (6%)
  starting transfers between devices  19.7 us (4%)
  other arithmetic  16.9 us (3%)
  local copies, waits for them, and re-layouts  16.8 us (3%)
  between operations  13.8 us (3%)
    unnamed x9, waiting for transfers between devices  216 us
    reduce_scatter x3, waiting for transfers between devices, per_device(): lax.psum_scatter(partial_sum.astype(jnp.bfloat16), 'col', scatter_dimensi...  87 us
    all_to_all x2, blocking collectives, per_device(): lax.all_to_all(jnp.stack([solved[level_idx - 1]] * lax.axis_size('row')),...  41.7 us
    all_gather x3, blocking collectives, per_device(): lax.all_gather(solution[level_idx + 1], 'col', axis=0, tiled=True)  39.8 us
    dot_general x3, matrix products, add_piece(): return jnp.dot(level_tile, shard_piece, preferred_element_type=jnp.float32)  12.8 us
    dot_general x3, matrix products, column_term(): lax.dot_general(level_tile, upper_blocks, (((0,), (0,)), ((), ())), prefe...  12.3 us
    slice x1, other arithmetic, per_device(): block_tile = lower_blocks[level_idx, 0, :, :, 0]  11.5 us
    all_to_all x1, starting transfers between devices, per_device(): lax.all_to_all(places.reshape(supernodes, group_rows), ('row', 'col'), sp...  11.1 us
  transfers between devices with their start and end apart: 9, of which 9 were waited for; matrix products, arithmetic and copies ran while one was open for 3% of the time, Pallas kernels for 0%

profile of v1, /device:TPU:0, one launch (start us, length us, event | category | flops | bytes accessed | tf_op | source)
XLA Modules:
  0.0 503.0 jit_solution(7804639576022549754)
XLA Ops:
  7.3 3.8 sort.17
  11.1 3.5 gather_fusion
  15.3 11.1 %all-to-all-start = ((s32[128,1,4]{2,1,0:T(1,128)}), s32[128,1,4]{2,1,0:T(1,128)S(1)}, u32[]{:S(2)}, u32[]{:S(2)}) async-start(s32[128,1,4]{2,1,0:T(1,128)} %bitcast), calls=%async_computation | async-start | bytes 131072 | tf_op jit(solution)/shard_map/all_to_all | solution.py:30
  26.5 1.6 gather_fusion.1
  28.8 7.2 %all-to-all-done = s32[128,1,4]{2,1,0:T(1,128)S(1)} async-done(((s32[128,1,4]{2,1,0:T(1,128)}), s32[128,1,4]{2,1,0:T(1,128)S(1)}, u32[]{:S(2)}, u32[]{:S(2)}) %all-to-all-start) | async-done | bytes 2080 | tf_op jit(solution)/shard_map/all_to_all | solution.py:30
  36.0 4.6 all-to-all-start.1
  42.1 9.5 %all-to-all-done.1 = bf16[128,4,256]{2,1,0:T(4,128)(2,1)S(1)} async-done(((bf16[128,4,256]{2,1,0:T(4,128)(2,1)}), bf16[128,4,256]{2,1,0:T(4,128)(2,1)S(1)}, u32[]{:S(2)}, u32[]{:S(2)}) %all-to-all-start.1) | async-done | bytes 262176 | tf_op jit(solution)/shard_map/all_to_all | solution.py:23
  51.6 2.4 scatter_custom_fusion
  54.3 1.1 stack.16
  55.4 3.7 all-to-all-start.2
  59.2 11.5 %fusion.67 = (bf16[1,1,8,128,1,16,128]{6,5,4,3,2,1,0:T(8,128)(2,1)}, bf16[1,1,8,128,1,16,128]{6,5,4,3,2,1,0:T(8,128)(2,1)}, bf16[1,1,8,128,1,16,128]{6,5,4,3,2,1...) fusion(bf16[3,1,8,128,1,16,128]{6,5,4,3,2,1,0:T(8,128)(2,1)} %p, ...), kind=kLoop, calls=%fused_computation.98 | loop fusion | flops 6291456 | bytes 37749504 | tf_op jit(solution)/shard_map/slice | solution.py:47
  70.7 5.8 %all-to-all-done.2 = bf16[16,128,256]{2,1,0:T(8,128)(2,1)S(1)} async-done(((bf16[16,128,256]{2,1,0:T(8,128)(2,1)}), bf16[16,128,256]{2,1,0:T(8,128)(2,1)S(1)}, u32[]{:S(2)}, u32[]{:S(2)}) %all-to-all-start.2) | async-done | bytes 1048608 | tf_op jit(solution)/shard_map/all_to_all | solution.py:67
  76.5 4.3 fusion.24
  80.9 27.7 %reduce-scatter.13.cloned.1.call-done = bf16[128,256]{1,0:T(8,128)(2,1)} async-done(((bf16[1024,256]{1,0:T(8,128)(2,1)}), bf16[128,256]{1,0:T(8,128)(2,1)}) %reduce-scatter.13.cloned.1.call-update) | async-done | bytes 65552 | tf_op jit(solution)/shard_map/reduce_scatter | solution.py:74
  108.6 1.0 fusion.34
  109.8 20.9 %all_to_all.29 = bf16[16,128,256]{2,1,0:T(8,128)(2,1)S(1)} all-to-all(bf16[16,128,256]{2,1,0:T(8,128)(2,1)S(1)} %stack.17), channel_id=1, replica_groups=mesh['row'=16,'col'=8] {'row'}, dimensions={0} | all-to-all | bytes 2097152 | tf_op jit(solution)/shard_map/all_to_all | solution.py:67
  130.7 4.2 fusion.27
  135.0 29.7 %reduce-scatter.15.cloned.1.call-done = bf16[128,256]{1,0:T(8,128)(2,1)} async-done(((bf16[1024,256]{1,0:T(8,128)(2,1)}), bf16[128,256]{1,0:T(8,128)(2,1)}) %reduce-scatter.15.cloned.1.call-update) | async-done | bytes 65552 | tf_op jit(solution)/shard_map/reduce_scatter | solution.py:74
  164.7 1.0 fusion.35
  166.0 20.9 %all_to_all.30 = bf16[16,128,256]{2,1,0:T(8,128)(2,1)S(1)} all-to-all(bf16[16,128,256]{2,1,0:T(8,128)(2,1)S(1)} %stack.18), channel_id=1, replica_groups=mesh['row'=16,'col'=8] {'row'}, dimensions={0} | all-to-all | bytes 2097152 | tf_op jit(solution)/shard_map/all_to_all | solution.py:67
  186.8 4.2 fusion.30
  191.1 29.7 %reduce-scatter.17.cloned.1.call-done = bf16[128,256]{1,0:T(8,128)(2,1)} async-done(((bf16[1024,256]{1,0:T(8,128)(2,1)}), bf16[128,256]{1,0:T(8,128)(2,1)}) %reduce-scatter.17.cloned.1.call-update) | async-done | bytes 65552 | tf_op jit(solution)/shard_map/reduce_scatter | solution.py:74
  220.8 1.2 convolution_convert_fusion.3
  222.0 12.6 %all_gather.9 = bf16[1024,256]{0,1:T(8,128)(2,1)S(1)} all-gather(bf16[128,256]{0,1:T(8,128)(2,1)S(1)} %bitcast.142), channel_id=1, replica_groups=mesh['row'=16,'col'=8] {'col'}, dimensions={0}, use_global_device_ids=true | all-gather | bytes 589824 | tf_op jit(solution)/shard_map/all_gather | solution.py:88
  235.1 4.2 fusion.23
  239.4 73.7 %reduce-scatter.19.cloned.1.call-done = bf16[128,256]{1,0:T(8,128)(2,1)} async-done(((bf16[2048,256]{1,0:T(8,128)(2,1)}), bf16[128,256]{1,0:T(8,128)(2,1)}) %reduce-scatter.19.cloned.1.call-update) | async-done | bytes 65552
  314.2 13.5 %all_gather.10 = bf16[1024,256]{0,1:T(8,128)(2,1)S(1)} all-gather(bf16[128,256]{0,1:T(8,128)(2,1)S(1)} %bitcast.144), channel_id=1, replica_groups=mesh['row'=16,'col'=8] {'col'}, dimensions={0}, use_global_device_ids=true | all-gather | bytes 589824 | tf_op jit(solution)/shard_map/all_gather | solution.py:88
  328.3 4.1 fusion.22
  332.4 71.1 %reduce-scatter.21.cloned.1.call-done = bf16[128,256]{1,0:T(8,128)(2,1)} async-done(((bf16[2048,256]{1,0:T(8,128)(2,1)}), bf16[128,256]{1,0:T(8,128)(2,1)}) %reduce-scatter.21.cloned.1.call-update) | async-done | bytes 65552
  404.6 13.7 %all_gather.11 = bf16[1024,256]{0,1:T(8,128)(2,1)S(1)} all-gather(bf16[128,256]{0,1:T(8,128)(2,1)S(1)} %bitcast.146), channel_id=1, replica_groups=mesh['row'=16,'col'=8] {'col'}, dimensions={0}, use_global_device_ids=true | all-gather | bytes 589824 | tf_op jit(solution)/shard_map/all_gather | solution.py:88
  419.0 4.1 fusion.21
  423.1 71.1 %reduce-scatter.23.cloned.1.call-done = bf16[128,256]{1,0:T(8,128)(2,1)} async-done(((bf16[2048,256]{1,0:T(8,128)(2,1)}), bf16[128,256]{1,0:T(8,128)(2,1)}) %reduce-scatter.23.cloned.1.call-update) | async-done | bytes 65552
  (56 shorter events, 10.8 us)
Async XLA Ops:
  6.5 19.9 %copy-start = (f32[512,256]{1,0:T(8,128)S(1)}, f32[512,256]{1,0:T(8,128)}, u32[]{:S(2)}) copy-start(f32[512,256]{1,0:T(8,128)} %param.5) | copy-start | bytes 1572868
  6.5 34.1 %copy-start.6 = (s32[3,1,8,1,16]{4,3,2,1,0:T(1,128)S(1)}, s32[3,1,8,1,16]{4,3,2,1,0:T(1,128)}, u32[]{:S(2)}) copy-start(s32[3,1,8,1,16]{4,3,2,1,0:T(1,128)} %param.9) | copy-start | bytes 4612
  6.5 47.4 %copy-start.5 = (bf16[4,1,128,128]{3,2,1,0:T(8,128)(2,1)S(1)}, bf16[4,1,128,128]{3,2,1,0:T(8,128)(2,1)}, u32[]{:S(2)}) copy-start(bf16[4,1,128,128]{3,2,1,0:T(8,128)(2,1)} %param.7) | copy-start | bytes 393220
  15.3 20.6 %all-to-all-start = ((s32[128,1,4]{2,1,0:T(1,128)}), s32[128,1,4]{2,1,0:T(1,128)S(1)}, u32[]{:S(2)}, u32[]{:S(2)}) async-start(s32[128,1,4]{2,1,0:T(1,128)} %bitcast), calls=%async_computation | async-start | bytes 131072 | tf_op jit(solution)/shard_map/all_to_all | solution.py:30
  36.0 15.6 %all-to-all-start.1 = ((bf16[128,4,256]{2,1,0:T(4,128)(2,1)}), bf16[128,4,256]{2,1,0:T(4,128)(2,1)S(1)}, u32[]{:S(2)}, u32[]{:S(2)}) async-start(bf16[128,4,256]{2,1,0:T(4,128)(2,1)} %convert_element_type.143), calls=%async_computation.1 | async-start | bytes 524288 | tf_op jit(solution)/shard_map/all_to_all | solution.py:23
  55.4 21.1 %all-to-all-start.2 = ((bf16[16,128,256]{2,1,0:T(8,128)(2,1)}), bf16[16,128,256]{2,1,0:T(8,128)(2,1)S(1)}, u32[]{:S(2)}, u32[]{:S(2)}) async-start(bf16[16,128,256]{2,1,0:T(8,128)(2,1)} %stack.16), calls=%async_computation.2 | async-start | bytes 2097152 | tf_op jit(solution)/shard_map/all_to_all | solution.py:67
  59.1 49.5 %reduce-scatter.13.cloned.1.call-start = ((), (), s32[]{:S(2)}) async-start(), calls=%async_computation.11 | async-start | bytes 589824 | tf_op jit(solution)/shard_map/reduce_scatter | solution.py:74
  80.8 83.9 %reduce-scatter.15.cloned.1.call-start = ((), (), s32[]{:S(2)}) async-start(), calls=%async_computation.12 | async-start | bytes 589824 | tf_op jit(solution)/shard_map/reduce_scatter | solution.py:74
  134.9 85.8 %reduce-scatter.17.cloned.1.call-start = ((), (), s32[]{:S(2)}) async-start(), calls=%async_computation.13 | async-start | bytes 589824 | tf_op jit(solution)/shard_map/reduce_scatter | solution.py:74
  191.1 122.0 %reduce-scatter.19.cloned.1.call-start = ((), (), s32[]{:S(2)}) async-start(), calls=%async_computation.14 | async-start | bytes 1114112
  222.0 13.2 %copy-start.4 = (bf16[1,1,8,128,1,16,128]{6,5,4,3,2,1,0:T(8,128)(2,1)S(1)}, bf16[1,1,8,128,1,16,128]{6,5,4,3,2,1,0:T(8,128)(2,1)}, u32[]{:S(2)}) copy-start(bf16[1,1,8,128,1,16,128]{6,5,4,3,2,1,0:T(8,128)(2,1)} %get-tuple-element.11) | copy-start | bytes 12582916
  239.3 164.2 %reduce-scatter.21.cloned.1.call-start = ((), (), s32[]{:S(2)}) async-start(), calls=%async_computation.15 | async-start | bytes 1114112
  314.0 14.3 %copy-start.3 = (bf16[1,1,8,128,1,16,128]{6,5,4,3,2,1,0:T(8,128)(2,1)S(1)}, bf16[1,1,8,128,1,16,128]{6,5,4,3,2,1,0:T(8,128)(2,1)}, u32[]{:S(2)}) copy-start(bf16[1,1,8,128,1,16,128]{6,5,4,3,2,1,0:T(8,128)(2,1)} %get-tuple-element.12) | copy-start | bytes 12582916
  332.4 161.8 %reduce-scatter.23.cloned.1.call-start = ((), (), s32[]{:S(2)}) async-start(), calls=%async_computation.16 | async-start | bytes 1114112
  404.5 14.5 %copy-start.2 = (bf16[1,1,8,128,1,16,128]{6,5,4,3,2,1,0:T(8,128)(2,1)S(1)}, bf16[1,1,8,128,1,16,128]{6,5,4,3,2,1,0:T(8,128)(2,1)}, u32[]{:S(2)}) copy-start(bf16[1,1,8,128,1,16,128]{6,5,4,3,2,1,0:T(8,128)(2,1)} %get-tuple-element.7) | copy-start | bytes 12582916
  419.0 77.2 %copy-start.1 = (f32[512,256]{1,0:T(8,128)S(1)}, f32[512,256]{1,0:T(8,128)}, u32[]{:S(2)}) copy-start(f32[512,256]{1,0:T(8,128)} %param.5) | copy-start | bytes 1572868
Sparse Core Ops, SparseCore 0:
  81.0 27.5 reduce-scatter.12
  135.1 29.5 reduce-scatter.14
  191.2 29.5 reduce-scatter.16
  239.4 73.5 reduce-scatter.18
  332.5 70.9 reduce-scatter.20
  423.2 70.9 reduce-scatter.22
